TPU v7x, 32 devices: a whole 2x2x4 slice. The times are simulated.
32 devices in a mesh: gx: 4 (over z), gy: 4 (over y, core), gz: 2 (over x).
Axes of the slice: x: 2, y: 2, z: 4, core: 2. Of those that a mesh axis runs over, the one named last changes fastest.
Arguments:
- node_irreps: bfloat16 [4, 4, 2, 16, 25, 128], P('gx', 'gy', 'gz'), may hold values from -5 to 11
- positions: float32 [4, 4, 2, 3, 16], P('gx', 'gy', 'gz'), may hold values from 0 to 6.8
- send_list: int32 [4, 4, 2, 8], P('gx', 'gy', 'gz'), may hold values from 0 to 15, as said below
- neighbours: int32 [4, 4, 2, 16, 32], P('gx', 'gy', 'gz'), may hold values from 0 to 231
- displacements: float32 [4, 4, 2, 3, 512], P('gx', 'gy', 'gz'), may hold values from -6 to 6
- order_zero: bfloat16 [640, 640], replicated, may hold values from -0.25 to 0.25
- order_one: bfloat16 [512, 1024], replicated, may hold values from -0.25 to 0.25
- order_two: bfloat16 [384, 768], replicated, may hold values from -0.3125 to 0.3125
- reciprocal_triples: int32 [1024, 3], replicated, may hold values from -6 to 6
- reciprocal_filter: float32 [1024, 128], replicated, may hold values from 0.1 to 1
- cotangent: float32 [4, 4, 2, 16, 128], P('gx', 'gy', 'gz'), may hold values from -5 to 11
Outputs:
- updated: bfloat16 [4, 4, 2, 16, 25, 128], P('gx', 'gy', 'gz')
- long_range: float32 [4, 4, 2, 16, 128], P('gx', 'gy', 'gz')
- charge_grad: float32 [4, 4, 2, 16, 128], P('gx', 'gy', 'gz')
- position_grad: float32 [4, 4, 2, 3, 16], P('gx', 'gy', 'gz')
Inputs may be any that keep to these rules, and one draw needn't show every extreme that they name: `send_list`: entries of one block are distinct atoms of that block.
All inputs are finite; a program needn't handle non-finite values.
Results may differ from a plain program's by a relative error of at most 0.0023.
Values may be sent and summed in bfloat16 or wider, within the bound.
No kernel may reach another device: no remote copies, remote signals or barrier semaphores. Data moves between devices by JAX's collectives and lax.ppermute only.
A program may use at most 64 MiB of HBM per device.

v0:
```python
import functools
import math

import jax
import jax.numpy as jnp
from jax import lax
from jax.experimental import pallas as pl
from jax.experimental.pallas import tpu as pltpu
from jax.sharding import PartitionSpec as P


AXES = ("gx", "gy", "gz")
cell_length = 6.8
planar_floor = 0.25
radial_width = 64.0
top_degree = 4
top_order = 2
bf16 = jnp.bfloat16
f32 = jnp.float32


def slot_of(degree, order):
    return degree * degree + degree + order


groups = [[slot_of(l, 0) for l in range(top_degree + 1)]]
for order in range(1, top_order + 1):
    groups.append([slot_of(l, sign * order) for sign in (1, -1) for l in range(order, top_degree + 1)])
slots = [slot for group in groups for slot in group]
slot_tiles = (len(slots) + 1) // 2
atom_tiles = 4


def leading(values):
    return values.astype(bf16)


def trailing(values):
    return (values - values.astype(bf16).astype(f32)).astype(bf16)


def cos_sin_turns(turns):
    rest = turns - jnp.round(turns)
    square = rest * rest
    cosine = jnp.full_like(square, cos_series[-1])
    for factor in cos_series[-2::-1]:
        cosine = cosine * square + factor
    sine = jnp.full_like(square, sin_series[-1])
    for factor in sin_series[-2::-1]:
        sine = sine * square + factor
    return cosine, sine * rest


def fitted(function, count):
    import numpy as np

    nodes = np.cos((np.arange(count) + 0.5) * np.pi / count)
    line = np.polynomial.chebyshev.chebfit(nodes, function((nodes + 1.0) / 8.0), count - 1)
    power = np.polynomial.chebyshev.cheb2poly(line)
    shift = np.polynomial.polynomial.Polynomial([-1.0, 8.0])
    total = np.polynomial.polynomial.Polynomial([0.0])
    for factor in power[::-1]:
        total = total * shift + factor
    return [float(factor) for factor in total.coef]


def _cos_of(s):
    import numpy as np

    return np.cos(2.0 * np.pi * np.sqrt(s))


def _sin_of(s):
    import numpy as np

    return np.sin(2.0 * np.pi * np.sqrt(s)) / np.sqrt(s)


cos_series = fitted(_cos_of, 7)
sin_series = fitted(_sin_of, 6)


def standing_row(row):
    count = row.shape[1]
    down = lax.broadcasted_iota(jnp.int32, (count, count), 0)
    across = lax.broadcasted_iota(jnp.int32, (count, count), 1)
    return jnp.sum(jnp.where(down == across, row, 0.0), axis=1, keepdims=True)


def lying_column(column):
    count = column.shape[0]
    down = lax.broadcasted_iota(jnp.int32, (count, count), 0)
    across = lax.broadcasted_iota(jnp.int32, (count, count), 1)
    return jnp.sum(jnp.where(down == across, column, 0.0), axis=0, keepdims=True)


def dot(left, right):
    return jnp.dot(left, right, preferred_element_type=f32)


def dot_nt(left, right):
    return lax.dot_general(left, right, (((1,), (1,)), ((), ())), preferred_element_type=f32)


def pack_kernel(sizes, *refs):
    far = refs[:4]
    tiles_ref = refs[4]
    near_refs = refs[5:9]
    arrivals = refs[9]
    copies = [pltpu.make_async_copy(a, b, arrivals.at[i]) for i, (a, b) in enumerate(zip(far, near_refs))]
    for copy in copies:
        copy.start()
    for copy in copies:
        copy.wait()
    send_ref, irreps_ref, places_ref, cotangent_ref = near_refs
    _, atoms, width = irreps_ref.shape
    offered = send_ref.shape[0]
    tiles_ref[0] = irreps_ref[0]
    cotangent = cotangent_ref[...]
    tiles_ref[1] = leading(cotangent)
    tiles_ref[2] = trailing(cotangent)
    lane = lax.broadcasted_iota(jnp.int32, (atoms, width), 1)
    packed = jnp.zeros((atoms, width), f32)
    for number, axis in enumerate(AXES):
        corner = lax.axis_index(axis).astype(f32)
        place = (places_ref[number] + cell_length * corner) / jnp.float32(cell_length * sizes[number])
        place = standing_row(place)
        high = place.astype(bf16).astype(f32)
        middle = (place - high).astype(bf16).astype(f32)
        low = (place - high) - middle
        for level, part in enumerate((high, middle, low)):
            packed = jnp.where(lane == 3 * level + number, part, packed)
    tiles_ref[3] = packed.astype(bf16)
    pick_row = lax.broadcasted_iota(jnp.int32, (offered, atoms), 0)
    pick_column = lax.broadcasted_iota(jnp.int32, (offered, atoms), 1)
    wanted = jnp.zeros((offered, atoms), jnp.int32)
    for position in range(offered):
        wanted = jnp.where(pick_row == position, send_ref[position], wanted)
    pick = jnp.where(wanted == pick_column, 1.0, 0.0).astype(bf16)
    rows = dot(pick, jnp.concatenate([irreps_ref[slot] for slot in slots], axis=1))
    for pair in range(slot_tiles):
        halves = []
        for number in (2 * pair, 2 * pair + 1):
            if number < len(slots):
                halves.append(rows[:, number * width : (number + 1) * width])
            else:
                halves.append(jnp.zeros((offered, width), f32))
        tiles_ref[atom_tiles + pair] = jnp.concatenate(halves, axis=0).astype(bf16)


def prepare_kernel(
    pieces, offered, neighbour_ref, displacement_ref, triples_ref, far_filter_ref, weights_ref, waves_ref, filter_ref, arrival
):
    waves = filter_ref.shape[0]
    shares = far_filter_ref.shape[0] // waves
    first_wave = pl.multiple_of((lax.axis_index("gy") % shares) * waves, waves)
    filter_copy = pltpu.make_async_copy(far_filter_ref.at[pl.ds(first_wave, waves), :], filter_ref, arrival)
    filter_copy.start()
    atoms, count = neighbour_ref.shape
    edges = atoms * count
    depth = weights_ref.shape[1]
    width = waves_ref.shape[1]
    first = displacement_ref[0]
    second = displacement_ref[1]
    third = displacement_ref[2]
    planar = first * first + second * second
    radial = jnp.exp(-(planar + third * third) / radial_width) / math.sqrt(count)
    turn = planar / (planar + planar_floor)
    slot = lax.broadcasted_iota(jnp.int32, (count, edges), 0)
    edge = lax.broadcasted_iota(jnp.int32, (count, edges), 1)
    repeat = jnp.where(edge % count == slot, 1.0, 0.0)
    spread = jnp.dot(
        neighbour_ref[...].astype(f32), repeat, precision=lax.Precision.HIGHEST, preferred_element_type=f32
    )
    owner = lax.broadcasted_iota(jnp.int32, (atoms, edges), 0)
    mine = owner == lax.broadcasted_iota(jnp.int32, (atoms, edges), 1) // count
    index = jnp.sum(jnp.where(mine, spread, 0.0), axis=0, keepdims=True).astype(jnp.int32)
    group = (index - atoms) // offered
    place = (index - atoms) - offered * group
    shift_x = (group >= 9).astype(jnp.int32) + (group >= 18).astype(jnp.int32)
    group = group - 9 * shift_x
    shift_y = (group >= 3).astype(jnp.int32) + (group >= 6).astype(jnp.int32)
    shift_z = group - 3 * shift_y
    line = jnp.zeros_like(index)
    for axis, shift, reach in reversed(tuple(zip(AXES, (shift_x, shift_y, shift_z), pieces))):
        if reach == 2:
            piece = jnp.where(shift == 1, 0, 1)
        else:
            odd = lax.axis_index(axis) % 2
            piece = jnp.where(shift == 1, 0, jnp.where(shift == 2, 1 + odd, 2 - odd))
        line = line * reach + piece
    rows = jnp.where(index < atoms, index, atoms + offered * line + place)
    hits = jnp.where(rows == lax.broadcasted_iota(jnp.int32, (depth, edges), 0), 1.0, 0.0).astype(bf16)
    strengths = [jnp.where(mine, strength, 0.0) for strength in (radial, radial * turn, radial * turn * turn)]
    strengths = jnp.concatenate(strengths, axis=0)
    both = dot_nt(jnp.concatenate([leading(strengths), trailing(strengths)], axis=0), hits)
    total = both[: len(groups) * atoms] + both[len(groups) * atoms :]
    for order in range(len(groups)):
        part = total[order * atoms : (order + 1) * atoms]
        weights_ref[2 * order * atoms : 2 * (order + 1) * atoms, :] = jnp.concatenate(
            [leading(part), trailing(part)], axis=0
        )
    triples = triples_ref[:, pl.ds(first_wave, waves)].astype(f32)
    triples = jnp.concatenate([triples, jnp.zeros((5, triples.shape[1]), f32)], axis=0)
    component = lax.broadcasted_iota(jnp.int32, (8, width), 0)
    lane = lax.broadcasted_iota(jnp.int32, (8, width), 1)
    chosen = jnp.where((lane % 3 == component) & (lane < 9), 1.0, 0.0)
    waves_ref[...] = lax.dot_general(
        triples.astype(bf16), chosen.astype(bf16), (((0,), (0,)), ((), ())), preferred_element_type=f32
    ).astype(bf16)
    filter_copy.wait()


def ewald_kernel(atom_spots, recipients, shares, wave_step, *refs):
    count_in = 1 + max(spot[0] for spot in atom_spots)
    arrived = refs[:count_in]
    waves_ref, filter_ref = refs[count_in : count_in + 2]
    part_refs = refs[count_in + 2 : count_in + 2 + shares]
    raw_ref, lead_ref, trail_ref, spot_ref, product_ref = refs[count_in + 2 + shares :]
    atoms, width = arrived[0].shape[1:]
    waves = filter_ref.shape[0]
    total_atoms = raw_ref.shape[0]

    where = 0
    for source, first, blocks in atom_spots:
        ref = arrived[source]

        def place_block(ref, start, row):
            rows = pl.ds(row, atoms)
            raw_ref[rows, :] = ref[start]
            lead_ref[rows, width:] = ref[start + 1]
            trail_ref[rows, width:] = ref[start + 2]
            spot_ref[rows, :] = ref[start + 3]

        if blocks <= 32:
            for block in range(blocks):
                place_block(ref, first + block * atom_tiles, where + block * atoms)
        else:

            def place_many(block, carry, ref=ref, first=first, where=where):
                place_block(ref, first + block * atom_tiles, pl.multiple_of(where + block * atoms, atoms))
                return carry

            lax.fori_loop(0, blocks, place_many, 0)
        where += blocks * atoms
    charges = raw_ref[...].astype(f32)
    mean = jnp.sum(charges, axis=0, keepdims=True) / total_atoms
    centered = charges - mean
    lead_ref[:, :width] = leading(centered)
    trail_ref[:, :width] = trailing(centered)

    def wave_rows(step):
        return slice(step * wave_step, (step + 1) * wave_step)

    chunk = min(total_atoms, 512)
    mean_total = jnp.zeros((1, width), f32)
    for step in range(waves // wave_step):

        def add_chunk(part, carry):
            factors, plane = carry
            rows = pl.ds(part * chunk, chunk) if isinstance(part, int) else pl.ds(pl.multiple_of(part * chunk, chunk), chunk)
            turns = dot_nt(waves_ref[wave_rows(step), :], spot_ref[rows, :])
            cosine, sine = cos_sin_turns(turns)
            both = jnp.concatenate([cosine, sine], axis=0)
            high = leading(both)
            low = trailing(both)
            factors = factors + (
                dot(high, lead_ref[rows, :]) + dot(high, trail_ref[rows, :]) + dot(low, lead_ref[rows, :])
            )
            return factors, plane + jnp.sum(both, axis=1, keepdims=True)

        start = (jnp.zeros((2 * wave_step, 2 * width), f32), jnp.zeros((2 * wave_step, 1), f32))
        if total_atoms == chunk:
            factors, plane = add_chunk(0, start)
        else:
            factors, plane = lax.fori_loop(0, total_atoms // chunk, add_chunk, start)
        strength = filter_ref[wave_rows(step), :]
        strength = jnp.concatenate([strength, strength], axis=0)
        strength = jnp.concatenate([strength, strength], axis=1)
        product = strength * factors
        mean_total = mean_total + jnp.sum(plane * product[:, width:], axis=0, keepdims=True)
        product_ref[0, step] = leading(product)
        product_ref[1, step] = trailing(product)

    def of_recipients(ref):
        return jnp.concatenate([ref[row : row + atoms, :] for row in recipients], axis=0)

    count = shares * atoms
    spots = of_recipients(spot_ref)
    swapped = []
    for ref in (lead_ref, trail_ref):
        pair = of_recipients(ref)
        swapped.append(jnp.concatenate([pair[:, width:], pair[:, :width]], axis=1))
    pair = jnp.concatenate(swapped, axis=0)
    terms = jnp.zeros((count, 2 * width), f32)
    pushed = jnp.zeros((2 * count, width), f32)
    for step in range(waves // wave_step):
        cosine, sine = cos_sin_turns(dot_nt(spots, waves_ref[wave_rows(step), :]))
        tables = jnp.concatenate([cosine, sine], axis=1)
        tables = jnp.concatenate([leading(tables), trailing(tables)], axis=0)
        high = product_ref[0, step]
        low = product_ref[1, step]
        both = dot(tables, high)
        terms = terms + both[:count] + both[count:] + dot(tables[:count], low)
        both = dot_nt(pair, high)
        against = both[:count] + both[count:] + dot_nt(pair[:count], low)
        slope = cosine * against[:, wave_step:] - sine * against[:, :wave_step]
        slope = jnp.concatenate([leading(slope), trailing(slope)], axis=0)
        pushed = pushed + dot(slope, waves_ref[wave_rows(step), :])
    charge = terms[:, width:] - mean_total / total_atoms
    pushed = pushed[:count] + pushed[count:]
    for number, ref in enumerate(part_refs):
        rows = slice(number * atoms, (number + 1) * atoms)
        ref[0] = terms[rows, :width]
        ref[1] = charge[rows]
        ref[2] = pushed[rows]


def edge_kernel(sizes, scale, halo_spots, part_count, *refs):
    count_in = 1 + max(spot[0] for spot in halo_spots)
    arrived = refs[:count_in]
    part_refs = refs[count_in : count_in + part_count]
    irreps_ref, weights_ref, zero_ref, one_ref, two_ref = refs[count_in + part_count : count_in + part_count + 5]
    updated_ref, long_ref, charge_ref, place_ref, table_ref = refs[count_in + part_count + 5 :]
    harmonics, atoms, width = irreps_ref.shape
    offered = atoms // 2

    sums = []
    for number in range(3):
        total = part_refs[0][number]
        for ref in part_refs[1:]:
            total = total + ref[number]
        sums.append(scale * total)
    long_ref[...] = sums[0]
    charge_ref[...] = sums[1]
    for number, size in enumerate(sizes):
        factor = 2.0 * math.pi / (cell_length * size)
        place_ref[number] = factor * lying_column(sums[2][:, number : number + 1])

    used = atoms + offered * len(halo_spots)
    if len(halo_spots) % 2:
        used -= offered
    table_ref[used:, :] = jnp.zeros((table_ref.shape[0] - used, table_ref.shape[1]), bf16)
    for number, slot in enumerate(slots):
        table_ref[:atoms, number * width : (number + 1) * width] = irreps_ref[slot]
    for first in range(0, len(halo_spots), 2):
        for tile in range(slot_tiles):
            wide = [arrived[source][start + tile].astype(f32) for source, start in halo_spots[first : first + 2]]
            if len(wide) == 1:
                wide.append(jnp.zeros((atoms, width), f32))
            for half in range(2):
                number = 2 * tile + half
                if number < len(slots):
                    rows = slice(half * offered, (half + 1) * offered)
                    table_ref[
                        atoms + first * offered : atoms + (first + 2) * offered, number * width : (number + 1) * width
                    ] = jnp.concatenate([wide[0][rows], wide[1][rows]], axis=0).astype(bf16)
    outputs = {}
    lane = 0
    for order, (group, mixing_ref) in enumerate(zip(groups, (zero_ref, one_ref, two_ref))):
        span = len(group) * width
        both = dot(weights_ref[2 * order * atoms : 2 * (order + 1) * atoms, :], table_ref[:, lane : lane + span])
        lane += span
        gathered = both[:atoms] + both[atoms:]
        if order == 0:
            both = dot(jnp.concatenate([leading(gathered), trailing(gathered)], axis=0), mixing_ref[...])
            mixed = both[:atoms] + both[atoms:]
        else:
            half = span // 2
            plus, minus = gathered[:, :half], gathered[:, half:]
            both = dot(
                jnp.concatenate([leading(plus), leading(minus), trailing(plus), trailing(minus)], axis=0),
                mixing_ref[...],
            )
            both = both[: 2 * atoms] + both[2 * atoms :]
            mixed = jnp.concatenate(
                [both[:atoms, :half] - both[atoms:, half:], both[atoms:, :half] + both[:atoms, half:]], axis=1
            )
        for number, slot in enumerate(group):
            outputs[slot] = mixed[:, number * width : (number + 1) * width]
    for slot in range(harmonics):
        if slot in outputs:
            updated_ref[slot] = (irreps_ref[slot].astype(f32) + outputs[slot]).astype(bf16)
        else:
            updated_ref[slot] = irreps_ref[slot]


def swap(value, sizes, partner):
    perm = []
    for x in range(sizes[0]):
        for y in range(sizes[1]):
            for z in range(sizes[2]):
                a, b, c = partner(x, y, z)
                perm.append(((x * sizes[1] + y) * sizes[2] + z, (a * sizes[1] + b) * sizes[2] + c))
    return lax.ppermute(value, AXES, perm)


def pair_of(index, size):
    return index ^ 1


def other_of(index, size):
    return (index - 1) % size if index % 2 == 0 else (index + 1) % size


def exchange(tiles, sizes):
    size_x, size_y, size_z = sizes
    if size_x == 4 and size_y == 4 and size_z == 2:
        paired = swap(tiles, sizes, lambda x, y, z: (x ^ 1, y, z))
        crossed = swap(jnp.concatenate([tiles[:atom_tiles], paired]), sizes, lambda x, y, z: (x ^ 2, y, z))
        atoms = jnp.concatenate([tiles[:atom_tiles], paired[:atom_tiles], crossed[: 2 * atom_tiles]])
        halo = jnp.concatenate([tiles[atom_tiles:], paired[atom_tiles:], crossed[2 * atom_tiles :]])

        def by_y(x, y, z):
            return (x, y ^ 3, z)

        def by_z(x, y, z):
            return (x, y, z ^ 1)

        def by_both(x, y, z):
            return (x, y ^ 3, z ^ 1)

        def by_core(x, y, z):
            return (x, y ^ 1, z)

        far = [swap(atoms, sizes, by_y), swap(atoms, sizes, by_z)]
        far = jnp.concatenate(far + [swap(atoms, sizes, by_both)])
        atom_arrays = [atoms, far, swap(atoms, sizes, by_core), swap(far, sizes, by_core)]
        halo_y = swap(halo, sizes, by_y)
        halo_z = swap(halo, sizes, by_z)
        halo_both = swap(halo, sizes, by_both)
        halo_core = swap(halo, sizes, by_core)
        halo_z_core = swap(halo_z, sizes, by_core)
        halo_arrays = [halo, halo_core, halo_y, halo_z, halo_z_core, halo_both]
        atom_spots = [(number, 0, array.shape[0] // atom_tiles) for number, array in enumerate(atom_arrays)]
        halo_spots = [(number, slot_tiles * piece) for number in range(6) for piece in range(3)]
        total_rows = sum(spot[2] for spot in atom_spots) * tiles.shape[1]
        return atom_arrays, atom_spots, halo_arrays, halo_spots, (0, total_rows // 2)
    everyone = lax.all_gather(tiles[:atom_tiles], AXES, axis=0, tiled=True)
    everyone = jnp.roll(everyone, -lax.axis_index(AXES) * atom_tiles, axis=0)
    layers = [tiles[atom_tiles:]]
    for number in range(3):
        arrived = []
        for partner in (pair_of, other_of)[: 1 if sizes[number] == 2 else 2]:

            def step(*place, number=number, partner=partner):
                place = list(place)
                place[number] = partner(place[number], sizes[number])
                return place

            arrived += [swap(part, sizes, step) for part in layers]
        layers = layers + arrived
    return [everyone], [(0, 0, math.prod(sizes))], layers, [(number, 0) for number in range(len(layers))], (0,)


def vmem():
    return pl.BlockSpec(memory_space=pltpu.VMEM)


def far():
    return pl.BlockSpec(memory_space=pltpu.HBM)


def grant(mebibytes):
    return pltpu.CompilerParams(vmem_limit_bytes=mebibytes * 2**20)


def stay(value):
    return pltpu.with_memory_space_constraint(value, pltpu.HBM)


def near(value):
    return pltpu.with_memory_space_constraint(value, pltpu.VMEM)


def layer(
    node_irreps,
    positions,
    send_list,
    neighbours,
    displacements,
    order_zero,
    order_one,
    order_two,
    reciprocal_triples,
    reciprocal_filter,
    cotangent,
):
    sizes = tuple(lax.axis_size(axis) for axis in AXES)
    irreps = jnp.transpose(node_irreps[0, 0, 0], (1, 0, 2))
    harmonics, atoms, width = irreps.shape
    sent = send_list[0, 0, 0]
    offered = sent.shape[0]
    neighbour = neighbours[0, 0, 0]
    waves = reciprocal_filter.shape[0]
    total_atoms = atoms * math.prod(sizes)
    own_cotangent = cotangent[0, 0, 0]

    tiles = pl.pallas_call(
        functools.partial(pack_kernel, sizes),
        out_shape=jax.ShapeDtypeStruct((atom_tiles + slot_tiles, atoms, width), bf16),
        in_specs=[far() for _ in range(4)],
        out_specs=vmem(),
        scratch_shapes=[
            pltpu.SMEM(sent.shape, jnp.int32),
            pltpu.VMEM(irreps.shape, bf16),
            pltpu.VMEM((3, 1, atoms), f32),
            pltpu.VMEM(own_cotangent.shape, f32),
            pltpu.SemaphoreType.DMA((4,)),
        ],
        compiler_params=grant(4),
        name="pack",
    )(*map(stay, (sent, irreps, positions[0, 0, 0][:, None, :], own_cotangent)))

    atom_arrays, atom_spots, halo_arrays, halo_spots, recipients = exchange(tiles, sizes)
    shares = len(recipients)
    pieces = tuple(2 if size == 2 else 3 for size in sizes)
    depth = -(-(atoms + offered * math.prod(pieces)) // 256) * 256

    weights, spread, strengths = pl.pallas_call(
        functools.partial(prepare_kernel, pieces, offered),
        out_shape=(
            jax.ShapeDtypeStruct((2 * len(groups) * atoms, depth), bf16),
            jax.ShapeDtypeStruct((waves // shares, width), bf16),
            jax.ShapeDtypeStruct((waves // shares, width), f32),
        ),
        in_specs=[vmem(), vmem(), vmem(), far()],
        out_specs=(vmem(), vmem(), vmem()),
        scratch_shapes=[pltpu.SemaphoreType.DMA],
        compiler_params=grant(6),
        name="prepare",
    )(
        *map(near, (neighbour, displacements[0, 0, 0][:, None, :], reciprocal_triples.T)), stay(reciprocal_filter)
    )

    wave_step = 128
    part_shape = jax.ShapeDtypeStruct((3, atoms, width), f32)
    parts = pl.pallas_call(
        functools.partial(ewald_kernel, tuple(atom_spots), recipients, shares, wave_step),
        out_shape=[part_shape] * shares,
        in_specs=[vmem() for _ in range(len(atom_arrays) + 2)],
        out_specs=[vmem()] * shares,
        scratch_shapes=[
            pltpu.VMEM((total_atoms, width), bf16),
            pltpu.VMEM((total_atoms, 2 * width), bf16),
            pltpu.VMEM((total_atoms, 2 * width), bf16),
            pltpu.VMEM((total_atoms, width), bf16),
            pltpu.VMEM((2, waves // shares // wave_step, 2 * wave_step, 2 * width), bf16),
        ],
        compiler_params=grant(12 + total_atoms // 256),
        name="ewald",
    )(*map(near, (*atom_arrays, spread, strengths)))
    parts = list(parts)
    if shares > 1:
        parts[1] = swap(parts[1], sizes, lambda x, y, z: (x, y ^ 1, z))

    scale = 1.0 / math.sqrt(total_atoms * waves)
    updated, long_range, charge_grad, position_grad = pl.pallas_call(
        functools.partial(edge_kernel, sizes, scale, tuple(halo_spots), shares),
        out_shape=(
            jax.ShapeDtypeStruct((harmonics, atoms, width), bf16),
            jax.ShapeDtypeStruct((atoms, width), f32),
            jax.ShapeDtypeStruct((atoms, width), f32),
            jax.ShapeDtypeStruct((3, 1, atoms), f32),
        ),
        in_specs=[vmem() for _ in range(len(halo_arrays) + shares + 5)],
        out_specs=tuple(vmem() for _ in range(4)),
        scratch_shapes=[pltpu.VMEM((depth, len(slots) * width), bf16)],
        compiler_params=grant(12),
        name="edges",
    )(*map(near, (*halo_arrays, *parts, irreps, weights, order_zero, order_one, order_two)))
    outs = (jnp.transpose(updated, (1, 0, 2)), long_range, charge_grad, position_grad[:, 0, :])
    return tuple(out[None, None, None] for out in outs)


def solution(mesh):
    return jax.shard_map(
        layer,
        mesh=mesh,
        in_specs=(
            P("gx", "gy", "gz", None, None, None),
            P("gx", "gy", "gz", None, None),
            P("gx", "gy", "gz", None),
            P("gx", "gy", "gz", None, None),
            P("gx", "gy", "gz", None, None),
            P(),
            P(),
            P(),
            P(),
            P(),
            P("gx", "gy", "gz", None, None),
        ),
        out_specs=(
            P("gx", "gy", "gz", None, None, None),
            P("gx", "gy", "gz", None, None),
            P("gx", "gy", "gz", None, None),
            P("gx", "gy", "gz", None, None),
        ),
        check_vma=False,
    )
```

profile of v0, /device:TPU:0, one launch (start us, length us, event | category | flops | bytes accessed | tf_op | source)
XLA Modules:
  0.0 31.2 jit_solution(754949062298802817)
XLA Ops:
  0.6 1.1 %pack.1 = bf16[14,16,128]{2,1,0:T(8,128)(2,1)S(1)} custom-call(s32[8]{0:T(128)} %bitcast.24, bf16[25,16,128]{2,1,0:T(8,128)(2,1)} %bitcast.17, f32[3,1,16]{2,1,0:T(1,128)} %bitcast.23, f32[16,128]{1,0:T(8,128)} %bitcast.22), custom_call_target="tpu_custom_call" | custom-call | tf_op jit(solution)/shard_map/pack/pallas_call | solution.py:499
  1.7 3.1 %collective-permute-start = (bf16[14,16,128]{2,1,0:T(8,128)(2,1)S(1)}, bf16[14,16,128]{2,1,0:T(8,128)(2,1)S(1)}, u32[]{:S(2)}, u32[]{:S(2)}) collective-permute-start(bf16[14,16,128]{2,1,0:T(8,128)(2,1)S(1)} %pack.1), channel_id=1, source_target_pairs={{0,8},{1,9},{2,10},{3,11},{4,12},{5,13},{6,14},{7,15},{8,0},{9,1},... | collective-permute-start | bytes 172040 | tf_op jit(solution)/shard_map/ppermute | solution.py:395
  4.9 2.2 %collective-permute-done = bf16[14,16,128]{2,1,0:T(8,128)(2,1)S(1)} collective-permute-done((bf16[14,16,128]{2,1,0:T(8,128)(2,1)S(1)}, bf16[14,16,128]{2,1,0:T(8,128)(2,1)S(1)}, u32[]{:S(2)}, u32[]{:S(2)}) %collective-permute-start) | collective-permute-done | bytes 57376 | tf_op jit(solution)/shard_map/ppermute | solution.py:395
  7.0 3.1 %collective-permute-start.1 = (bf16[18,16,128]{2,1,0:T(8,128)(2,1)S(1)}, bf16[18,16,128]{2,1,0:T(8,128)(2,1)S(1)}, u32[]{:S(2)}, u32[]{:S(2)}) collective-permute-start(bf16[18,16,128]{2,1,0:T(8,128)(2,1)S(1)} %pad_maximum_fusion.1), channel_id=1, source_target_pairs={{0,16},{1,17},{2,18},{3,19},{4,20},{5,21},{6,22},{7,23},{8,24},{9,... | collective-permute-start | bytes 221192 | tf_op jit(solution)/shard_map/ppermute | solution.py:395
  10.1 0.0 copy-start.3
  10.1 0.0 copy-start.6
  10.1 0.0 copy-start.2
  10.2 2.3 %collective-permute-done.1 = bf16[18,16,128]{2,1,0:T(8,128)(2,1)S(1)} collective-permute-done((bf16[18,16,128]{2,1,0:T(8,128)(2,1)S(1)}, bf16[18,16,128]{2,1,0:T(8,128)(2,1)S(1)}, u32[]{:S(2)}, u32[]{:S(2)}) %collective-permute-start.1) | collective-permute-done | bytes 73760 | tf_op jit(solution)/shard_map/ppermute | solution.py:395
  12.5 0.1 collective-permute-start.7
  12.5 1.9 %collective-permute-start.8 = (bf16[16,16,128]{2,1,0:T(8,128)(2,1)S(1)}, bf16[16,16,128]{2,1,0:T(8,128)(2,1)S(1)}, u32[]{:S(2)}, u32[]{:S(2)}) collective-permute-start(bf16[16,16,128]{2,1,0:T(8,128)(2,1)S(1)} %pad_maximum_fusion.2.refs_0_), channel_id=1, source_target_pairs={{0,1},{1,0},{2,3},{3,2},{4,5},{5,4},{6,7},{7,6},{8,9},{9,8},{10,11... | collective-permute-start | bytes 196616 | tf_op jit(solution)/shard_map/ppermute | solution.py:395
  14.4 1.1 %collective-permute-start.9 = (bf16[16,16,128]{2,1,0:T(8,128)(2,1)S(1)}, bf16[16,16,128]{2,1,0:T(8,128)(2,1)S(1)}, u32[]{:S(2)}, u32[]{:S(2)}) collective-permute-start(bf16[16,16,128]{2,1,0:T(8,128)(2,1)S(1)} %pad_maximum_fusion.2.refs_0_), channel_id=1, source_target_pairs={{0,7},{1,6},{2,5},{3,4},{4,3},{5,2},{6,1},{7,0},{8,15},{9,14},{10,... | collective-permute-start | bytes 196616 | tf_op jit(solution)/shard_map/ppermute | solution.py:395
  15.5 0.0 copy-start.4
  15.5 0.0 copy-start.5
  15.5 0.0 copy-start
  15.6 1.8 %collective-permute-start.4 = (bf16[30,16,128]{2,1,0:T(8,128)(2,1)S(1)}, bf16[30,16,128]{2,1,0:T(8,128)(2,1)S(1)}, u32[]{:S(2)}, u32[]{:S(2)}) collective-permute-start(bf16[30,16,128]{2,1,0:T(8,128)(2,1)S(1)} %pad_maximum_fusion.refs_0_), channel_id=1, source_target_pairs={{0,1},{1,0},{2,3},{3,2},{4,5},{5,4},{6,7},{7,6},{8,9},{9,8},{10,11... | collective-permute-start | bytes 368648 | tf_op jit(solution)/shard_map/ppermute | solution.py:395
  17.4 0.0 collective-permute-done.7
  17.4 0.0 collective-permute-done.8
  17.4 0.0 copy-start.1
  17.4 1.6 %collective-permute-done.9 = bf16[16,16,128]{2,1,0:T(8,128)(2,1)S(1)} collective-permute-done((bf16[16,16,128]{2,1,0:T(8,128)(2,1)S(1)}, bf16[16,16,128]{2,1,0:T(8,128)(2,1)S(1)}, u32[]{:S(2)}, u32[]{:S(2)}) %collective-permute-start.9) | collective-permute-done | bytes 65568 | tf_op jit(solution)/shard_map/ppermute | solution.py:395
  19.0 1.9 %collective-permute-start.11 = (bf16[48,16,128]{2,1,0:T(8,128)(2,1)S(1)}, bf16[48,16,128]{2,1,0:T(8,128)(2,1)S(1)}, u32[]{:S(2)}, u32[]{:S(2)}) collective-permute-start(bf16[48,16,128]{2,1,0:T(8,128)(2,1)S(1)} %constant_dynamic-update-slice_fusion.refs_1_), channel_id=1, source_target_pairs={{0,2},{1,3},{2,0},{3,1},{4,6},{5,7},{6,4},{7,5},{8,10},{9,11},{10,... | collective-permute-start | bytes 589832 | tf_op jit(solution)/shard_map/ppermute | solution.py:395
  20.9 0.1 collective-permute-start.10
  21.0 0.4 %collective-permute-start.2 = (bf16[30,16,128]{2,1,0:T(8,128)(2,1)S(1)}, bf16[30,16,128]{2,1,0:T(8,128)(2,1)S(1)}, u32[]{:S(2)}, u32[]{:S(2)}) collective-permute-start(bf16[30,16,128]{2,1,0:T(8,128)(2,1)S(1)} %pad_maximum_fusion.refs_0_), channel_id=1, source_target_pairs={{0,2},{1,3},{2,0},{3,1},{4,6},{5,7},{6,4},{7,5},{8,10},{9,11},{10,... | collective-permute-start | bytes 368648 | tf_op jit(solution)/shard_map/ppermute | solution.py:395
  21.5 0.3 %collective-permute-start.3 = (bf16[30,16,128]{2,1,0:T(8,128)(2,1)S(1)}, bf16[30,16,128]{2,1,0:T(8,128)(2,1)S(1)}, u32[]{:S(2)}, u32[]{:S(2)}) collective-permute-start(bf16[30,16,128]{2,1,0:T(8,128)(2,1)S(1)} %pad_maximum_fusion.refs_0_), channel_id=1, source_target_pairs={{0,6},{1,7},{2,4},{3,5},{4,2},{5,3},{6,0},{7,1},{8,14},{9,15},{10,... | collective-permute-start | bytes 368648 | tf_op jit(solution)/shard_map/ppermute | solution.py:395
  21.8 0.4 %collective-permute-done.10.refs_2_ = bf16[16,16,128]{2,1,0:T(8,128)(2,1)S(1)} collective-permute-done((bf16[16,16,128]{2,1,0:T(8,128)(2,1)S(1)}, bf16[16,16,128]{2,1,0:T(8,128)(2,1)S(1)}, u32[]{:S(2)}, u32[]{:S(2)}) %collective-permute-start.10) | collective-permute-done | bytes 65568 | tf_op jit(solution)/shard_map/ppermute | solution.py:395
  22.2 1.2 %collective-permute-start.6 = (bf16[30,16,128]{2,1,0:T(8,128)(2,1)S(1)}, bf16[30,16,128]{2,1,0:T(8,128)(2,1)S(1)}, u32[]{:S(2)}, u32[]{:S(2)}) collective-permute-start(bf16[30,16,128]{2,1,0:T(8,128)(2,1)S(1)} %pad_maximum_fusion.refs_0_), channel_id=1, source_target_pairs={{0,7},{1,6},{2,5},{3,4},{4,3},{5,2},{6,1},{7,0},{8,15},{9,14},{10,... | collective-permute-start | bytes 368648 | tf_op jit(solution)/shard_map/ppermute | solution.py:395
  23.4 0.0 collective-permute-done.4.refs_3_
  23.4 0.1 collective-permute-start.5
  23.4 0.0 copy-done.6
  23.4 0.0 copy-done.4
  23.4 0.0 copy-done.5
  23.4 1.1 %prepare.1 = (bf16[96,256]{1,0:T(8,128)(2,1)S(1)}, bf16[512,128]{1,0:T(8,128)(2,1)S(1)}, f32[512,128]{1,0:T(8,128)S(1)}) custom-call(s32[16,32]{1,0:T(8,128)S(1)} %bitcast.20, f32[3,1,512]{2,1,0:T(1,128)S(1)} %bitcast.21, s32[3,1024]{1,0:T(4,128)S(1)} %bitcast.19, f32[1024,128]{1,0:T(8,128)} %far_filter_ref.1), custom_call_target="tpu_custom_call" | custom-call | tf_op jit(solution)/shard_map/prepare/pallas_call | solution.py:520
  24.6 0.0 collective-permute-done.11.refs_3_
  24.6 3.0 %ewald.1 = (f32[3,16,128]{2,1,0:T(8,128)S(1)}, f32[3,16,128]{2,1,0:T(8,128)S(1)}) custom-call(bf16[16,16,128]{2,1,0:T(8,128)(2,1)S(1)} %pad_maximum_fusion.2.refs_0_, bf16[48,16,128]{2,1,0:T(8,128)(2,1)S(1)} %constant_dynamic-update-slice_fusion.refs_1_, bf16[16,16,128]{2,1,0:T(8,128)(2,1)S(1)} %collective-permute-done.10.refs_2_, ...), custom_call_target="tpu_custom_call" | custom-call | tf_op jit(solution)/shard_map/ewald/pallas_call | solution.py:538
  27.6 0.5 %collective-permute-start.12 = (f32[3,16,128]{2,1,0:T(8,128)S(1)}, f32[3,16,128]{2,1,0:T(8,128)S(1)}, u32[]{:S(2)}, u32[]{:S(2)}) collective-permute-start(f32[3,16,128]{2,1,0:T(8,128)S(1)} %get-tuple-element.16), channel_id=1, source_target_pairs={{0,2},{1,3},{2,0},{3,1},{4,6},{5,7},{6,4},{7,5},{8,10},{9,11},{10,... | collective-permute-start | bytes 73736 | tf_op jit(solution)/shard_map/ppermute | solution.py:395
  28.1 0.0 collective-permute-done.2.refs_1_
  28.1 1.4 %collective-permute-done.3.refs_2_ = bf16[30,16,128]{2,1,0:T(8,128)(2,1)S(1)} collective-permute-done((bf16[30,16,128]{2,1,0:T(8,128)(2,1)S(1)}, bf16[30,16,128]{2,1,0:T(8,128)(2,1)S(1)}, u32[]{:S(2)}, u32[]{:S(2)}) %collective-permute-start.3) | collective-permute-done | bytes 122912 | tf_op jit(solution)/shard_map/ppermute | solution.py:395
  29.4 0.0 collective-permute-done.6.refs_5_
  29.4 0.0 collective-permute-done.5.refs_4_
  29.5 0.0 collective-permute-done.12.refs_7_
  29.5 0.0 copy-done.3
  29.5 0.0 copy-done.2
  29.5 0.0 copy-done
  29.5 0.0 copy-done.1
  29.5 1.7 %edges.1 = (bf16[25,16,128]{2,1,0:T(8,128)(2,1)}, f32[16,128]{1,0:T(8,128)}, f32[16,128]{1,0:T(8,128)}, f32[3,1,16]{2,1,0:T(1,128)}) custom-call(bf16[30,16,128]{2,1,0:T(8,128)(2,1)S(1)} %pad_maximum_fusion.refs_0_, bf16[30,16,128]{2,1,0:T(8,128)(2,1)S(1)} %collective-permute-done.2.refs_1_, bf16[30,16,128]{2,1,0:T(8,128)(2,1)S(1)} %collective-permute-done.3.refs_2_, ...), custom_call_target="tpu_custom_call" | custom-call | tf_op jit(solution)/shard_map/edges/pallas_call | solution.py:558
  (12 shorter events, 0.1 us)
Async XLA Ops:
  1.7 5.3 %collective-permute-start = (bf16[14,16,128]{2,1,0:T(8,128)(2,1)S(1)}, bf16[14,16,128]{2,1,0:T(8,128)(2,1)S(1)}, u32[]{:S(2)}, u32[]{:S(2)}) collective-permute-start(bf16[14,16,128]{2,1,0:T(8,128)(2,1)S(1)} %pack.1), channel_id=1, source_target_pairs={{0,8},{1,9},{2,10},{3,11},{4,12},{5,13},{6,14},{7,15},{8,0},{9,1},... | collective-permute-start | bytes 172040 | tf_op jit(solution)/shard_map/ppermute | solution.py:395
  7.0 5.4 %collective-permute-start.1 = (bf16[18,16,128]{2,1,0:T(8,128)(2,1)S(1)}, bf16[18,16,128]{2,1,0:T(8,128)(2,1)S(1)}, u32[]{:S(2)}, u32[]{:S(2)}) collective-permute-start(bf16[18,16,128]{2,1,0:T(8,128)(2,1)S(1)} %pad_maximum_fusion.1), channel_id=1, source_target_pairs={{0,16},{1,17},{2,18},{3,19},{4,20},{5,21},{6,22},{7,23},{8,24},{9,... | collective-permute-start | bytes 221192 | tf_op jit(solution)/shard_map/ppermute | solution.py:395
  10.1 19.3 %copy-start.3 = (bf16[1,1,1,16,25,128]{5,3,4,2,1,0:T(8,128)(2,1)S(1)}, bf16[1,1,1,16,25,128]{5,3,4,2,1,0:T(8,128)(2,1)}, u32[]{:S(2)}) copy-start(bf16[1,1,1,16,25,128]{5,3,4,2,1,0:T(8,128)(2,1)} %param.11) | copy-start | bytes 307204
  10.1 13.3 %copy-start.6 = (f32[1,1,1,3,512]{4,2,3,1,0:T(1,128)S(1)}, f32[1,1,1,3,512]{4,2,3,1,0:T(1,128)}, u32[]{:S(2)}) copy-start(f32[1,1,1,3,512]{4,2,3,1,0:T(1,128)} %param.15) | copy-start | bytes 18436
  10.1 19.3 %copy-start.2 = (bf16[384,768]{1,0:T(8,128)(2,1)S(1)}, bf16[384,768]{1,0:T(8,128)(2,1)}, u32[]{:S(2)}) copy-start(bf16[384,768]{1,0:T(8,128)(2,1)} %refs_12_.1) | copy-start | bytes 1769476
  12.5 4.9 %collective-permute-start.7 = (bf16[16,16,128]{2,1,0:T(8,128)(2,1)S(1)}, bf16[16,16,128]{2,1,0:T(8,128)(2,1)S(1)}, u32[]{:S(2)}, u32[]{:S(2)}) collective-permute-start(bf16[16,16,128]{2,1,0:T(8,128)(2,1)S(1)} %pad_maximum_fusion.2.refs_0_), channel_id=1, source_target_pairs={{0,6},{1,7},{2,4},{3,5},{4,2},{5,3},{6,0},{7,1},{8,14},{9,15},{10,... | collective-permute-start | bytes 196616 | tf_op jit(solution)/shard_map/ppermute | solution.py:395
  12.5 4.9 %collective-permute-start.8 = (bf16[16,16,128]{2,1,0:T(8,128)(2,1)S(1)}, bf16[16,16,128]{2,1,0:T(8,128)(2,1)S(1)}, u32[]{:S(2)}, u32[]{:S(2)}) collective-permute-start(bf16[16,16,128]{2,1,0:T(8,128)(2,1)S(1)} %pad_maximum_fusion.2.refs_0_), channel_id=1, source_target_pairs={{0,1},{1,0},{2,3},{3,2},{4,5},{5,4},{6,7},{7,6},{8,9},{9,8},{10,11... | collective-permute-start | bytes 196616 | tf_op jit(solution)/shard_map/ppermute | solution.py:395
  14.4 4.6 %collective-permute-start.9 = (bf16[16,16,128]{2,1,0:T(8,128)(2,1)S(1)}, bf16[16,16,128]{2,1,0:T(8,128)(2,1)S(1)}, u32[]{:S(2)}, u32[]{:S(2)}) collective-permute-start(bf16[16,16,128]{2,1,0:T(8,128)(2,1)S(1)} %pad_maximum_fusion.2.refs_0_), channel_id=1, source_target_pairs={{0,7},{1,6},{2,5},{3,4},{4,3},{5,2},{6,1},{7,0},{8,15},{9,14},{10,... | collective-permute-start | bytes 196616 | tf_op jit(solution)/shard_map/ppermute | solution.py:395
  15.5 7.9 %copy-start.4 = (s32[1024,3]{0,1:T(4,128)S(1)}, s32[1024,3]{0,1:T(4,128)}, u32[]{:S(2)}) copy-start(s32[1024,3]{0,1:T(4,128)} %param.19) | copy-start | bytes 36868
  15.5 7.9 %copy-start.5 = (s32[1,1,1,16,32]{4,3,2,1,0:T(8,128)S(1)}, s32[1,1,1,16,32]{4,3,2,1,0:T(8,128)}, u32[]{:S(2)}) copy-start(s32[1,1,1,16,32]{4,3,2,1,0:T(8,128)} %param.14) | copy-start | bytes 6148
  15.5 13.9 %copy-start = (bf16[512,1024]{1,0:T(8,128)(2,1)S(1)}, bf16[512,1024]{1,0:T(8,128)(2,1)}, u32[]{:S(2)}) copy-start(bf16[512,1024]{1,0:T(8,128)(2,1)} %refs_11_.1) | copy-start | bytes 3145732
  15.6 7.8 %collective-permute-start.4 = (bf16[30,16,128]{2,1,0:T(8,128)(2,1)S(1)}, bf16[30,16,128]{2,1,0:T(8,128)(2,1)S(1)}, u32[]{:S(2)}, u32[]{:S(2)}) collective-permute-start(bf16[30,16,128]{2,1,0:T(8,128)(2,1)S(1)} %pad_maximum_fusion.refs_0_), channel_id=1, source_target_pairs={{0,1},{1,0},{2,3},{3,2},{4,5},{5,4},{6,7},{7,6},{8,9},{9,8},{10,11... | collective-permute-start | bytes 368648 | tf_op jit(solution)/shard_map/ppermute | solution.py:395
  17.4 12.1 %copy-start.1 = (bf16[640,640]{1,0:T(8,128)(2,1)S(1)}, bf16[640,640]{1,0:T(8,128)(2,1)}, u32[]{:S(2)}) copy-start(bf16[640,640]{1,0:T(8,128)(2,1)} %refs_10_.1) | copy-start | bytes 2457604
  19.0 5.6 %collective-permute-start.11 = (bf16[48,16,128]{2,1,0:T(8,128)(2,1)S(1)}, bf16[48,16,128]{2,1,0:T(8,128)(2,1)S(1)}, u32[]{:S(2)}, u32[]{:S(2)}) collective-permute-start(bf16[48,16,128]{2,1,0:T(8,128)(2,1)S(1)} %constant_dynamic-update-slice_fusion.refs_1_), channel_id=1, source_target_pairs={{0,2},{1,3},{2,0},{3,1},{4,6},{5,7},{6,4},{7,5},{8,10},{9,11},{10,... | collective-permute-start | bytes 589832 | tf_op jit(solution)/shard_map/ppermute | solution.py:395
  20.9 1.3 %collective-permute-start.10 = (bf16[16,16,128]{2,1,0:T(8,128)(2,1)S(1)}, bf16[16,16,128]{2,1,0:T(8,128)(2,1)S(1)}, u32[]{:S(2)}, u32[]{:S(2)}) collective-permute-start(bf16[16,16,128]{2,1,0:T(8,128)(2,1)S(1)} %pad_maximum_fusion.2.refs_0_), channel_id=1, source_target_pairs={{0,2},{1,3},{2,0},{3,1},{4,6},{5,7},{6,4},{7,5},{8,10},{9,11},{10,... | collective-permute-start | bytes 196616 | tf_op jit(solution)/shard_map/ppermute | solution.py:395
  21.0 7.1 %collective-permute-start.2 = (bf16[30,16,128]{2,1,0:T(8,128)(2,1)S(1)}, bf16[30,16,128]{2,1,0:T(8,128)(2,1)S(1)}, u32[]{:S(2)}, u32[]{:S(2)}) collective-permute-start(bf16[30,16,128]{2,1,0:T(8,128)(2,1)S(1)} %pad_maximum_fusion.refs_0_), channel_id=1, source_target_pairs={{0,2},{1,3},{2,0},{3,1},{4,6},{5,7},{6,4},{7,5},{8,10},{9,11},{10,... | collective-permute-start | bytes 368648 | tf_op jit(solution)/shard_map/ppermute | solution.py:395
  21.5 8.0 %collective-permute-start.3 = (bf16[30,16,128]{2,1,0:T(8,128)(2,1)S(1)}, bf16[30,16,128]{2,1,0:T(8,128)(2,1)S(1)}, u32[]{:S(2)}, u32[]{:S(2)}) collective-permute-start(bf16[30,16,128]{2,1,0:T(8,128)(2,1)S(1)} %pad_maximum_fusion.refs_0_), channel_id=1, source_target_pairs={{0,6},{1,7},{2,4},{3,5},{4,2},{5,3},{6,0},{7,1},{8,14},{9,15},{10,... | collective-permute-start | bytes 368648 | tf_op jit(solution)/shard_map/ppermute | solution.py:395
  22.2 7.3 %collective-permute-start.6 = (bf16[30,16,128]{2,1,0:T(8,128)(2,1)S(1)}, bf16[30,16,128]{2,1,0:T(8,128)(2,1)S(1)}, u32[]{:S(2)}, u32[]{:S(2)}) collective-permute-start(bf16[30,16,128]{2,1,0:T(8,128)(2,1)S(1)} %pad_maximum_fusion.refs_0_), channel_id=1, source_target_pairs={{0,7},{1,6},{2,5},{3,4},{4,3},{5,2},{6,1},{7,0},{8,15},{9,14},{10,... | collective-permute-start | bytes 368648 | tf_op jit(solution)/shard_map/ppermute | solution.py:395
  23.4 6.1 %collective-permute-start.5 = (bf16[30,16,128]{2,1,0:T(8,128)(2,1)S(1)}, bf16[30,16,128]{2,1,0:T(8,128)(2,1)S(1)}, u32[]{:S(2)}, u32[]{:S(2)}) collective-permute-start(bf16[30,16,128]{2,1,0:T(8,128)(2,1)S(1)} %collective-permute-done.4.refs_3_), channel_id=1, source_target_pairs={{0,2},{1,3},{2,0},{3,1},{4,6},{5,7},{6,4},{7,5},{8,10},{9,11},{10,... | collective-permute-start | bytes 368648 | tf_op jit(solution)/shard_map/ppermute | solution.py:395
  27.6 1.8 %collective-permute-start.12 = (f32[3,16,128]{2,1,0:T(8,128)S(1)}, f32[3,16,128]{2,1,0:T(8,128)S(1)}, u32[]{:S(2)}, u32[]{:S(2)}) collective-permute-start(f32[3,16,128]{2,1,0:T(8,128)S(1)} %get-tuple-element.16), channel_id=1, source_target_pairs={{0,2},{1,3},{2,0},{3,1},{4,6},{5,7},{6,4},{7,5},{8,10},{9,11},{10,... | collective-permute-start | bytes 73736 | tf_op jit(solution)/shard_map/ppermute | solution.py:395
where the time goes:
time: 31.3 us; the launch traced here: 31.2 us
  starting transfers between devices  15.5 us (50%)
  waiting for transfers between devices  7.81 us (25%)
  Pallas kernels  6.91 us (22%)
  between operations  0.79 us (3%)
    ppermute x13, starting transfers between devices, swap(): return lax.ppermute(value, AXES, perm)  15.5 us
    ppermute x13, waiting for transfers between devices, swap(): return lax.ppermute(value, AXES, perm)  7.81 us
    pallas_call x1, Pallas kernels, layer(): pl.pallas_call(functools.partial(ewald_kernel, tuple(atom_spots), recipie...  3 us
    pallas_call x1, Pallas kernels, layer(): pl.pallas_call(functools.partial(edge_kernel, sizes, scale, tuple(halo_sp...  1.67 us
    pallas_call x1, Pallas kernels, layer(): pl.pallas_call(functools.partial(prepare_kernel, pieces, offered), out_sh...  1.15 us
    pallas_call x1, Pallas kernels, layer(): pl.pallas_call(functools.partial(pack_kernel, sizes), out_shape=jax.Shape...  1.09 us
  transfers between devices with their start and end apart: 13, of which 5 were waited for; matrix products, arithmetic and copies ran while one was open for 0% of the time, Pallas kernels for 13%

commit v1 on v0

--- a/solution.py
+++ b/solution.py
@@ -27,8 +27,9 @@
 for order in range(1, top_order + 1):
     groups.append([slot_of(l, sign * order) for sign in (1, -1) for l in range(order, top_degree + 1)])
 slots = [slot for group in groups for slot in group]
-slot_tiles = (len(slots) + 1) // 2
+slot_tiles = len(slots) // 2
 atom_tiles = 4
+place_lanes = 16
 
 
 def leading(values):
@@ -119,8 +120,8 @@
     cotangent = cotangent_ref[...]
     tiles_ref[1] = leading(cotangent)
     tiles_ref[2] = trailing(cotangent)
-    lane = lax.broadcasted_iota(jnp.int32, (atoms, width), 1)
-    packed = jnp.zeros((atoms, width), f32)
+    lane = lax.broadcasted_iota(jnp.int32, (offered, width), 1)
+    packed = jnp.zeros((offered, width), f32)
     for number, axis in enumerate(AXES):
         corner = lax.axis_index(axis).astype(f32)
         place = (places_ref[number] + cell_length * corner) / jnp.float32(cell_length * sizes[number])
@@ -129,8 +130,9 @@
         middle = (place - high).astype(bf16).astype(f32)
         low = (place - high) - middle
         for level, part in enumerate((high, middle, low)):
-            packed = jnp.where(lane == 3 * level + number, part, packed)
-    tiles_ref[3] = packed.astype(bf16)
+            for half in range(atoms // offered):
+                rows = part[half * offered : (half + 1) * offered]
+                packed = jnp.where(lane == place_lanes * half + 3 * level + number, rows, packed)
     pick_row = lax.broadcasted_iota(jnp.int32, (offered, atoms), 0)
     pick_column = lax.broadcasted_iota(jnp.int32, (offered, atoms), 1)
     wanted = jnp.zeros((offered, atoms), jnp.int32)
@@ -138,14 +140,10 @@
         wanted = jnp.where(pick_row == position, send_ref[position], wanted)
     pick = jnp.where(wanted == pick_column, 1.0, 0.0).astype(bf16)
     rows = dot(pick, jnp.concatenate([irreps_ref[slot] for slot in slots], axis=1))
+    pieces = [rows[:, number * width : (number + 1) * width] for number in range(len(slots))]
+    tiles_ref[3] = jnp.concatenate([packed, pieces[-1]], axis=0).astype(bf16)
     for pair in range(slot_tiles):
-        halves = []
-        for number in (2 * pair, 2 * pair + 1):
-            if number < len(slots):
-                halves.append(rows[:, number * width : (number + 1) * width])
-            else:
-                halves.append(jnp.zeros((offered, width), f32))
-        tiles_ref[atom_tiles + pair] = jnp.concatenate(halves, axis=0).astype(bf16)
+        tiles_ref[atom_tiles + pair] = jnp.concatenate(pieces[2 * pair : 2 * pair + 2], axis=0).astype(bf16)
 
 
 def prepare_kernel(
@@ -204,7 +202,8 @@
     triples = jnp.concatenate([triples, jnp.zeros((5, triples.shape[1]), f32)], axis=0)
     component = lax.broadcasted_iota(jnp.int32, (8, width), 0)
     lane = lax.broadcasted_iota(jnp.int32, (8, width), 1)
-    chosen = jnp.where((lane % 3 == component) & (lane < 9), 1.0, 0.0)
+    part = lane % place_lanes
+    chosen = jnp.where((part % 3 == component) & (part < 9) & (lane < 2 * place_lanes), 1.0, 0.0)
     waves_ref[...] = lax.dot_general(
         triples.astype(bf16), chosen.astype(bf16), (((0,), (0,)), ((), ())), preferred_element_type=f32
     ).astype(bf16)
@@ -221,6 +220,7 @@
     waves = filter_ref.shape[0]
     total_atoms = raw_ref.shape[0]
 
+    upper = lax.broadcasted_iota(jnp.int32, (atoms // 2, width), 1) < place_lanes
     where = 0
     for source, first, blocks in atom_spots:
         ref = arrived[source]
@@ -230,7 +230,10 @@
             raw_ref[rows, :] = ref[start]
             lead_ref[rows, width:] = ref[start + 1]
             trail_ref[rows, width:] = ref[start + 2]
-            spot_ref[rows, :] = ref[start + 3]
+            places = ref[start + 3].astype(f32)[: atoms // 2]
+            spot_ref[rows, :] = jnp.concatenate(
+                [jnp.where(upper, places, 0.0), jnp.where(upper, 0.0, places)], axis=0
+            ).astype(bf16)
 
         if blocks <= 32:
             for block in range(blocks):
@@ -317,7 +320,7 @@
 
 
 def edge_kernel(sizes, scale, halo_spots, part_count, *refs):
-    count_in = 1 + max(spot[0] for spot in halo_spots)
+    count_in = len(refs) - part_count - 10
     arrived = refs[:count_in]
     part_refs = refs[count_in : count_in + part_count]
     irreps_ref, weights_ref, zero_ref, one_ref, two_ref = refs[count_in + part_count : count_in + part_count + 5]
@@ -343,18 +346,22 @@
     table_ref[used:, :] = jnp.zeros((table_ref.shape[0] - used, table_ref.shape[1]), bf16)
     for number, slot in enumerate(slots):
         table_ref[:atoms, number * width : (number + 1) * width] = irreps_ref[slot]
+
+    def put(first, number, pieces):
+        if len(pieces) == 1:
+            pieces = pieces + [jnp.zeros((offered, width), f32)]
+        table_ref[
+            atoms + first * offered : atoms + (first + 2) * offered, number * width : (number + 1) * width
+        ] = jnp.concatenate(pieces, axis=0).astype(bf16)
+
     for first in range(0, len(halo_spots), 2):
+        spots = halo_spots[first : first + 2]
         for tile in range(slot_tiles):
-            wide = [arrived[source][start + tile].astype(f32) for source, start in halo_spots[first : first + 2]]
-            if len(wide) == 1:
-                wide.append(jnp.zeros((atoms, width), f32))
-            for half in range(2):
-                number = 2 * tile + half
-                if number < len(slots):
-                    rows = slice(half * offered, (half + 1) * offered)
-                    table_ref[
-                        atoms + first * offered : atoms + (first + 2) * offered, number * width : (number + 1) * width
-                    ] = jnp.concatenate([wide[0][rows], wide[1][rows]], axis=0).astype(bf16)
+            wide = [arrived[source][start + tile].astype(f32) for source, start, _, _ in spots]
+            put(first, 2 * tile, [piece[:offered] for piece in wide])
+            put(first, 2 * tile + 1, [piece[offered:] for piece in wide])
+        wide = [arrived[source][tile].astype(f32) for _, _, source, tile in spots]
+        put(first, len(slots) - 1, [piece[offered:] for piece in wide])
     outputs = {}
     lane = 0
     for order, (group, mixing_ref) in enumerate(zip(groups, (zero_ref, one_ref, two_ref))):
@@ -407,9 +414,10 @@
     size_x, size_y, size_z = sizes
     if size_x == 4 and size_y == 4 and size_z == 2:
         paired = swap(tiles, sizes, lambda x, y, z: (x ^ 1, y, z))
-        crossed = swap(jnp.concatenate([tiles[:atom_tiles], paired]), sizes, lambda x, y, z: (x ^ 2, y, z))
-        atoms = jnp.concatenate([tiles[:atom_tiles], paired[:atom_tiles], crossed[: 2 * atom_tiles]])
-        halo = jnp.concatenate([tiles[atom_tiles:], paired[atom_tiles:], crossed[2 * atom_tiles :]])
+        across = swap(tiles, sizes, lambda x, y, z: (x ^ 3, y, z))
+        skipped = swap(tiles[:atom_tiles], sizes, lambda x, y, z: (x ^ 2, y, z))
+        atoms = jnp.concatenate([tiles[:atom_tiles], paired[:atom_tiles], skipped, across[:atom_tiles]])
+        halo = jnp.concatenate([tiles[atom_tiles:], paired[atom_tiles:], across[atom_tiles:]])
 
         def by_y(x, y, z):
             return (x, y ^ 3, z)
@@ -433,12 +441,17 @@
         halo_z_core = swap(halo_z, sizes, by_core)
         halo_arrays = [halo, halo_core, halo_y, halo_z, halo_z_core, halo_both]
         atom_spots = [(number, 0, array.shape[0] // atom_tiles) for number, array in enumerate(atom_arrays)]
-        halo_spots = [(number, slot_tiles * piece) for number in range(6) for piece in range(3)]
+        beside = ((0, 0), (2, 0), (1, 0), (1, 4 * atom_tiles), (3, 4 * atom_tiles), (1, 8 * atom_tiles))
+        halo_spots = [
+            (number, slot_tiles * piece, len(halo_arrays) + source, first + atom_tiles * block + atom_tiles - 1)
+            for number, (source, first) in enumerate(beside)
+            for piece, block in enumerate((0, 1, 3))
+        ]
         total_rows = sum(spot[2] for spot in atom_spots) * tiles.shape[1]
-        return atom_arrays, atom_spots, halo_arrays, halo_spots, (0, total_rows // 2)
+        return atom_arrays, atom_spots, halo_arrays + atom_arrays, halo_spots, (0, total_rows // 2)
     everyone = lax.all_gather(tiles[:atom_tiles], AXES, axis=0, tiled=True)
     everyone = jnp.roll(everyone, -lax.axis_index(AXES) * atom_tiles, axis=0)
-    layers = [tiles[atom_tiles:]]
+    layers = [tiles[atom_tiles - 1 :]]
     for number in range(3):
         arrived = []
         for partner in (pair_of, other_of)[: 1 if sizes[number] == 2 else 2]:
@@ -450,7 +463,7 @@
 
             arrived += [swap(part, sizes, step) for part in layers]
         layers = layers + arrived
-    return [everyone], [(0, 0, math.prod(sizes))], layers, [(number, 0) for number in range(len(layers))], (0,)
+    return [everyone], [(0, 0, math.prod(sizes))], layers, [(number, 1, number, 0) for number in range(len(layers))], (0,)
 
 
 def vmem():

time: 31.3 us -> 32.2 us (1.029)
  waiting for transfers between devices: 7.81 us -> 9.91 us
  starting transfers between devices: 15.5 us -> 14.2 us
    ppermute x13 -> x14, waiting for transfers between devices: 7.81 us -> 9.91 us  [swap(): return lax.ppermute(value, AXES, perm)]
    ppermute x13 -> x14, starting transfers between devices: 15.5 us -> 14.2 us  [swap(): return lax.ppermute(value, AXES, perm)]
  transfers between devices with their start and end apart: 13 -> 14, of which waited for: 5 -> 7; matrix products, arithmetic and copies ran while one was open for 0% -> 0% of each run, Pallas kernels for 13% -> 13%
where the time goes in v1:
time: 32.2 us; the launch traced here: 32 us
  starting transfers between devices  14.2 us (44%)
  waiting for transfers between devices  9.91 us (31%)
  Pallas kernels  6.98 us (22%)
  between operations  0.76 us (2%)
    ppermute x14, starting transfers between devices, swap(): return lax.ppermute(value, AXES, perm)  14.2 us
    ppermute x14, waiting for transfers between devices, swap(): return lax.ppermute(value, AXES, perm)  9.91 us
    pallas_call x1, Pallas kernels, layer(): pl.pallas_call(functools.partial(ewald_kernel, tuple(atom_spots), recipie...  3 us
    pallas_call x1, Pallas kernels, layer(): pl.pallas_call(functools.partial(edge_kernel, sizes, scale, tuple(halo_sp...  1.68 us
    pallas_call x1, Pallas kernels, layer(): pl.pallas_call(functools.partial(pack_kernel, sizes), out_shape=jax.Shape...  1.15 us
    pallas_call x1, Pallas kernels, layer(): pl.pallas_call(functools.partial(prepare_kernel, pieces, offered), out_sh...  1.15 us
  transfers between devices with their start and end apart: 14, of which 7 were waited for; matrix products, arithmetic and copies ran while one was open for 0% of the time, Pallas kernels for 13%

profile of v1, /device:TPU:0, one launch (start us, length us, event | category | flops | bytes accessed | tf_op | source)
XLA Modules:
  0.0 32.0 jit_solution(16162821099822361155)
XLA Ops:
  0.6 0.0 copy-start.3
  0.6 1.1 %pack.1 = bf16[13,16,128]{2,1,0:T(8,128)(2,1)S(1)} custom-call(s32[8]{0:T(128)} %bitcast.24, bf16[25,16,128]{2,1,0:T(8,128)(2,1)} %bitcast.17, f32[3,1,16]{2,1,0:T(1,128)} %bitcast.23, f32[16,128]{1,0:T(8,128)} %bitcast.22), custom_call_target="tpu_custom_call" | custom-call | tf_op jit(solution)/shard_map/pack/pallas_call | solution.py:512
  1.8 3.1 %collective-permute-start = (bf16[13,16,128]{2,1,0:T(8,128)(2,1)S(1)}, bf16[13,16,128]{2,1,0:T(8,128)(2,1)S(1)}, u32[]{:S(2)}, u32[]{:S(2)}) collective-permute-start(bf16[13,16,128]{2,1,0:T(8,128)(2,1)S(1)} %pack.1), channel_id=1, source_target_pairs={{0,8},{1,9},{2,10},{3,11},{4,12},{5,13},{6,14},{7,15},{8,0},{9,1},... | collective-permute-start | bytes 159752 | tf_op jit(solution)/shard_map/ppermute | solution.py:402
  4.9 2.5 %collective-permute-start.1 = (bf16[13,16,128]{2,1,0:T(8,128)(2,1)S(1)}, bf16[13,16,128]{2,1,0:T(8,128)(2,1)S(1)}, u32[]{:S(2)}, u32[]{:S(2)}) collective-permute-start(bf16[13,16,128]{2,1,0:T(8,128)(2,1)S(1)} %pack.1), channel_id=1, source_target_pairs={{0,24},{1,25},{2,26},{3,27},{4,28},{5,29},{6,30},{7,31},{8,16},{9,... | collective-permute-start | bytes 159752 | tf_op jit(solution)/shard_map/ppermute | solution.py:402
  7.4 0.1 collective-permute-start.7
  7.5 0.0 collective-permute-done
  7.5 0.0 copy-start.6
  7.5 3.6 %collective-permute-done.1 = bf16[13,16,128]{2,1,0:T(8,128)(2,1)S(1)} collective-permute-done((bf16[13,16,128]{2,1,0:T(8,128)(2,1)S(1)}, bf16[13,16,128]{2,1,0:T(8,128)(2,1)S(1)}, u32[]{:S(2)}, u32[]{:S(2)}) %collective-permute-start.1) | collective-permute-done | bytes 53280 | tf_op jit(solution)/shard_map/ppermute | solution.py:402
  11.1 0.0 copy-start.2
  11.1 1.0 %collective-permute-done.7 = bf16[4,16,128]{2,1,0:T(8,128)(2,1)S(1)} collective-permute-done((bf16[4,16,128]{2,1,0:T(8,128)(2,1)S(1)}, bf16[4,16,128]{2,1,0:T(8,128)(2,1)S(1)}, u32[]{:S(2)}, u32[]{:S(2)}) %collective-permute-start.7) | collective-permute-done | bytes 16416 | tf_op jit(solution)/shard_map/ppermute | solution.py:402
  12.1 0.1 collective-permute-start.8
  12.2 1.6 %collective-permute-start.9 = (bf16[16,16,128]{2,1,0:T(8,128)(2,1)S(1)}, bf16[16,16,128]{2,1,0:T(8,128)(2,1)S(1)}, u32[]{:S(2)}, u32[]{:S(2)}) collective-permute-start(bf16[16,16,128]{2,1,0:T(8,128)(2,1)S(1)} %pad_maximum_fusion.1.refs_0_.refs_6_), channel_id=1, source_target_pairs={{0,1},{1,0},{2,3},{3,2},{4,5},{5,4},{6,7},{7,6},{8,9},{9,8},{10,11... | collective-permute-start | bytes 196616 | tf_op jit(solution)/shard_map/ppermute | solution.py:402
  13.7 1.4 %collective-permute-start.10 = (bf16[16,16,128]{2,1,0:T(8,128)(2,1)S(1)}, bf16[16,16,128]{2,1,0:T(8,128)(2,1)S(1)}, u32[]{:S(2)}, u32[]{:S(2)}) collective-permute-start(bf16[16,16,128]{2,1,0:T(8,128)(2,1)S(1)} %pad_maximum_fusion.1.refs_0_.refs_6_), channel_id=1, source_target_pairs={{0,7},{1,6},{2,5},{3,4},{4,3},{5,2},{6,1},{7,0},{8,15},{9,14},{10,... | collective-permute-start | bytes 196616 | tf_op jit(solution)/shard_map/ppermute | solution.py:402
  15.1 0.0 copy-start.4
  15.1 0.0 copy-start.5
  15.1 0.0 copy-start
  15.1 1.3 %collective-permute-done.8 = bf16[16,16,128]{2,1,0:T(8,128)(2,1)S(1)} collective-permute-done((bf16[16,16,128]{2,1,0:T(8,128)(2,1)S(1)}, bf16[16,16,128]{2,1,0:T(8,128)(2,1)S(1)}, u32[]{:S(2)}, u32[]{:S(2)}) %collective-permute-start.8) | collective-permute-done | bytes 65568 | tf_op jit(solution)/shard_map/ppermute | solution.py:402
  16.4 0.2 collective-permute-done.9
  16.6 1.8 %collective-permute-done.10 = bf16[16,16,128]{2,1,0:T(8,128)(2,1)S(1)} collective-permute-done((bf16[16,16,128]{2,1,0:T(8,128)(2,1)S(1)}, bf16[16,16,128]{2,1,0:T(8,128)(2,1)S(1)}, u32[]{:S(2)}, u32[]{:S(2)}) %collective-permute-start.10) | collective-permute-done | bytes 65568 | tf_op jit(solution)/shard_map/ppermute | solution.py:402
  18.4 0.0 copy-start.1
  18.4 1.2 %collective-permute-start.12 = (bf16[48,16,128]{2,1,0:T(8,128)(2,1)S(1)}, bf16[48,16,128]{2,1,0:T(8,128)(2,1)S(1)}, u32[]{:S(2)}, u32[]{:S(2)}) collective-permute-start(bf16[48,16,128]{2,1,0:T(8,128)(2,1)S(1)} %constant_dynamic-update-slice_fusion.refs_1_.refs_7_), channel_id=1, source_target_pairs={{0,2},{1,3},{2,0},{3,1},{4,6},{5,7},{6,4},{7,5},{8,10},{9,11},{10,... | collective-permute-start | bytes 589832 | tf_op jit(solution)/shard_map/ppermute | solution.py:402
  19.7 0.9 %collective-permute-start.4 = (bf16[27,16,128]{2,1,0:T(8,128)(2,1)S(1)}, bf16[27,16,128]{2,1,0:T(8,128)(2,1)S(1)}, u32[]{:S(2)}, u32[]{:S(2)}) collective-permute-start(bf16[27,16,128]{2,1,0:T(8,128)(2,1)S(1)} %pad_maximum_fusion.refs_0_), channel_id=1, source_target_pairs={{0,1},{1,0},{2,3},{3,2},{4,5},{5,4},{6,7},{7,6},{8,9},{9,8},{10,11... | collective-permute-start | bytes 331784 | tf_op jit(solution)/shard_map/ppermute | solution.py:402
  20.6 0.0 collective-permute-start.11
  20.6 0.5 %collective-permute-start.2 = (bf16[27,16,128]{2,1,0:T(8,128)(2,1)S(1)}, bf16[27,16,128]{2,1,0:T(8,128)(2,1)S(1)}, u32[]{:S(2)}, u32[]{:S(2)}) collective-permute-start(bf16[27,16,128]{2,1,0:T(8,128)(2,1)S(1)} %pad_maximum_fusion.refs_0_), channel_id=1, source_target_pairs={{0,2},{1,3},{2,0},{3,1},{4,6},{5,7},{6,4},{7,5},{8,10},{9,11},{10,... | collective-permute-start | bytes 331784 | tf_op jit(solution)/shard_map/ppermute | solution.py:402
  21.1 1.0 %collective-permute-start.3 = (bf16[27,16,128]{2,1,0:T(8,128)(2,1)S(1)}, bf16[27,16,128]{2,1,0:T(8,128)(2,1)S(1)}, u32[]{:S(2)}, u32[]{:S(2)}) collective-permute-start(bf16[27,16,128]{2,1,0:T(8,128)(2,1)S(1)} %pad_maximum_fusion.refs_0_), channel_id=1, source_target_pairs={{0,6},{1,7},{2,4},{3,5},{4,2},{5,3},{6,0},{7,1},{8,14},{9,15},{10,... | collective-permute-start | bytes 331784 | tf_op jit(solution)/shard_map/ppermute | solution.py:402
  22.1 0.0 collective-permute-done.11.refs_2_.refs_8_
  22.1 1.4 %collective-permute-start.6 = (bf16[27,16,128]{2,1,0:T(8,128)(2,1)S(1)}, bf16[27,16,128]{2,1,0:T(8,128)(2,1)S(1)}, u32[]{:S(2)}, u32[]{:S(2)}) collective-permute-start(bf16[27,16,128]{2,1,0:T(8,128)(2,1)S(1)} %pad_maximum_fusion.refs_0_), channel_id=1, source_target_pairs={{0,7},{1,6},{2,5},{3,4},{4,3},{5,2},{6,1},{7,0},{8,15},{9,14},{10,... | collective-permute-start | bytes 331784 | tf_op jit(solution)/shard_map/ppermute | solution.py:402
  23.5 1.3 %collective-permute-done.4.refs_3_ = bf16[27,16,128]{2,1,0:T(8,128)(2,1)S(1)} collective-permute-done((bf16[27,16,128]{2,1,0:T(8,128)(2,1)S(1)}, bf16[27,16,128]{2,1,0:T(8,128)(2,1)S(1)}, u32[]{:S(2)}, u32[]{:S(2)}) %collective-permute-start.4) | collective-permute-done | bytes 110624 | tf_op jit(solution)/shard_map/ppermute | solution.py:402
  24.7 0.0 collective-permute-start.5
  24.7 0.0 copy-done.6
  24.7 0.0 copy-done.4
  24.7 0.0 copy-done.5
  24.7 1.1 %prepare.1 = (bf16[96,256]{1,0:T(8,128)(2,1)S(1)}, bf16[512,128]{1,0:T(8,128)(2,1)S(1)}, f32[512,128]{1,0:T(8,128)S(1)}) custom-call(s32[16,32]{1,0:T(8,128)S(1)} %bitcast.20, f32[3,1,512]{2,1,0:T(1,128)S(1)} %bitcast.21, s32[3,1024]{1,0:T(4,128)S(1)} %bitcast.19, f32[1024,128]{1,0:T(8,128)} %far_filter_ref.1), custom_call_target="tpu_custom_call" | custom-call | tf_op jit(solution)/shard_map/prepare/pallas_call | solution.py:533
  25.9 0.0 collective-permute-done.12.refs_3_.refs_9_
  25.9 3.0 %ewald.1 = (f32[3,16,128]{2,1,0:T(8,128)S(1)}, f32[3,16,128]{2,1,0:T(8,128)S(1)}) custom-call(bf16[16,16,128]{2,1,0:T(8,128)(2,1)S(1)} %pad_maximum_fusion.1.refs_0_.refs_6_, bf16[48,16,128]{2,1,0:T(8,128)(2,1)S(1)} %constant_dynamic-update-slice_fusion.refs_1_.refs_7_, bf16[16,16,128]{2,1,0:T(8,128)(2,1)S(1)} %collective-permute-done.11.refs_2_.refs_8_, ...), custom_call_target="tpu_custom_call" | custom-call | tf_op jit(solution)/shard_map/ewald/pallas_call | solution.py:551
  28.9 0.5 %collective-permute-start.13 = (f32[3,16,128]{2,1,0:T(8,128)S(1)}, f32[3,16,128]{2,1,0:T(8,128)S(1)}, u32[]{:S(2)}, u32[]{:S(2)}) collective-permute-start(f32[3,16,128]{2,1,0:T(8,128)S(1)} %get-tuple-element.16), channel_id=1, source_target_pairs={{0,2},{1,3},{2,0},{3,1},{4,6},{5,7},{6,4},{7,5},{8,10},{9,11},{10,... | collective-permute-start | bytes 73736 | tf_op jit(solution)/shard_map/ppermute | solution.py:402
  29.4 0.0 collective-permute-done.2.refs_1_
  29.5 0.0 collective-permute-done.3.refs_2_
  29.5 0.0 collective-permute-done.6.refs_5_
  29.5 0.0 collective-permute-done.5.refs_4_
  29.5 0.8 %collective-permute-done.13.refs_11_ = f32[3,16,128]{2,1,0:T(8,128)S(1)} collective-permute-done((f32[3,16,128]{2,1,0:T(8,128)S(1)}, f32[3,16,128]{2,1,0:T(8,128)S(1)}, u32[]{:S(2)}, u32[]{:S(2)}) %collective-permute-start.13) | collective-permute-done | bytes 24608 | tf_op jit(solution)/shard_map/ppermute | solution.py:402
  30.3 0.0 copy-done.3
  30.3 0.0 copy-done.2
  30.3 0.0 copy-done
  30.3 0.0 copy-done.1
  30.3 1.7 %edges.1 = (bf16[25,16,128]{2,1,0:T(8,128)(2,1)}, f32[16,128]{1,0:T(8,128)}, f32[16,128]{1,0:T(8,128)}, f32[3,1,16]{2,1,0:T(1,128)}) custom-call(bf16[27,16,128]{2,1,0:T(8,128)(2,1)S(1)} %pad_maximum_fusion.refs_0_, bf16[27,16,128]{2,1,0:T(8,128)(2,1)S(1)} %collective-permute-done.2.refs_1_, bf16[27,16,128]{2,1,0:T(8,128)(2,1)S(1)} %collective-permute-done.3.refs_2_, ...), custom_call_target="tpu_custom_call" | custom-call | tf_op jit(solution)/shard_map/edges/pallas_call | solution.py:571
  (11 shorter events, 0.1 us)
Async XLA Ops:
  0.6 29.7 %copy-start.3 = (bf16[1,1,1,16,25,128]{5,3,4,2,1,0:T(8,128)(2,1)S(1)}, bf16[1,1,1,16,25,128]{5,3,4,2,1,0:T(8,128)(2,1)}, u32[]{:S(2)}) copy-start(bf16[1,1,1,16,25,128]{5,3,4,2,1,0:T(8,128)(2,1)} %param.11) | copy-start | bytes 307204
  1.8 5.7 %collective-permute-start = (bf16[13,16,128]{2,1,0:T(8,128)(2,1)S(1)}, bf16[13,16,128]{2,1,0:T(8,128)(2,1)S(1)}, u32[]{:S(2)}, u32[]{:S(2)}) collective-permute-start(bf16[13,16,128]{2,1,0:T(8,128)(2,1)S(1)} %pack.1), channel_id=1, source_target_pairs={{0,8},{1,9},{2,10},{3,11},{4,12},{5,13},{6,14},{7,15},{8,0},{9,1},... | collective-permute-start | bytes 159752 | tf_op jit(solution)/shard_map/ppermute | solution.py:402
  4.9 6.2 %collective-permute-start.1 = (bf16[13,16,128]{2,1,0:T(8,128)(2,1)S(1)}, bf16[13,16,128]{2,1,0:T(8,128)(2,1)S(1)}, u32[]{:S(2)}, u32[]{:S(2)}) collective-permute-start(bf16[13,16,128]{2,1,0:T(8,128)(2,1)S(1)} %pack.1), channel_id=1, source_target_pairs={{0,24},{1,25},{2,26},{3,27},{4,28},{5,29},{6,30},{7,31},{8,16},{9,... | collective-permute-start | bytes 159752 | tf_op jit(solution)/shard_map/ppermute | solution.py:402
  7.4 4.6 %collective-permute-start.7 = (bf16[4,16,128]{2,1,0:T(8,128)(2,1)S(1)}, bf16[4,16,128]{2,1,0:T(8,128)(2,1)S(1)}, u32[]{:S(2)}, u32[]{:S(2)}) collective-permute-start(bf16[4,16,128]{2,1,0:T(8,128)(2,1)S(1)} %slice.28), channel_id=1, source_target_pairs={{0,16},{1,17},{2,18},{3,19},{4,20},{5,21},{6,22},{7,23},{8,24},{9,... | collective-permute-start | bytes 49160 | tf_op jit(solution)/shard_map/ppermute | solution.py:402
  7.5 17.2 %copy-start.6 = (f32[1,1,1,3,512]{4,2,3,1,0:T(1,128)S(1)}, f32[1,1,1,3,512]{4,2,3,1,0:T(1,128)}, u32[]{:S(2)}) copy-start(f32[1,1,1,3,512]{4,2,3,1,0:T(1,128)} %param.15) | copy-start | bytes 18436
  11.1 19.2 %copy-start.2 = (bf16[384,768]{1,0:T(8,128)(2,1)S(1)}, bf16[384,768]{1,0:T(8,128)(2,1)}, u32[]{:S(2)}) copy-start(bf16[384,768]{1,0:T(8,128)(2,1)} %refs_16_.1) | copy-start | bytes 1769476
  12.1 4.4 %collective-permute-start.8 = (bf16[16,16,128]{2,1,0:T(8,128)(2,1)S(1)}, bf16[16,16,128]{2,1,0:T(8,128)(2,1)S(1)}, u32[]{:S(2)}, u32[]{:S(2)}) collective-permute-start(bf16[16,16,128]{2,1,0:T(8,128)(2,1)S(1)} %pad_maximum_fusion.1.refs_0_.refs_6_), channel_id=1, source_target_pairs={{0,6},{1,7},{2,4},{3,5},{4,2},{5,3},{6,0},{7,1},{8,14},{9,15},{10,... | collective-permute-start | bytes 196616 | tf_op jit(solution)/shard_map/ppermute | solution.py:402
  12.2 4.5 %collective-permute-start.9 = (bf16[16,16,128]{2,1,0:T(8,128)(2,1)S(1)}, bf16[16,16,128]{2,1,0:T(8,128)(2,1)S(1)}, u32[]{:S(2)}, u32[]{:S(2)}) collective-permute-start(bf16[16,16,128]{2,1,0:T(8,128)(2,1)S(1)} %pad_maximum_fusion.1.refs_0_.refs_6_), channel_id=1, source_target_pairs={{0,1},{1,0},{2,3},{3,2},{4,5},{5,4},{6,7},{7,6},{8,9},{9,8},{10,11... | collective-permute-start | bytes 196616 | tf_op jit(solution)/shard_map/ppermute | solution.py:402
  13.7 4.7 %collective-permute-start.10 = (bf16[16,16,128]{2,1,0:T(8,128)(2,1)S(1)}, bf16[16,16,128]{2,1,0:T(8,128)(2,1)S(1)}, u32[]{:S(2)}, u32[]{:S(2)}) collective-permute-start(bf16[16,16,128]{2,1,0:T(8,128)(2,1)S(1)} %pad_maximum_fusion.1.refs_0_.refs_6_), channel_id=1, source_target_pairs={{0,7},{1,6},{2,5},{3,4},{4,3},{5,2},{6,1},{7,0},{8,15},{9,14},{10,... | collective-permute-start | bytes 196616 | tf_op jit(solution)/shard_map/ppermute | solution.py:402
  15.1 9.7 %copy-start.4 = (s32[1024,3]{0,1:T(4,128)S(1)}, s32[1024,3]{0,1:T(4,128)}, u32[]{:S(2)}) copy-start(s32[1024,3]{0,1:T(4,128)} %param.19) | copy-start | bytes 36868
  15.1 9.7 %copy-start.5 = (s32[1,1,1,16,32]{4,3,2,1,0:T(8,128)S(1)}, s32[1,1,1,16,32]{4,3,2,1,0:T(8,128)}, u32[]{:S(2)}) copy-start(s32[1,1,1,16,32]{4,3,2,1,0:T(8,128)} %param.14) | copy-start | bytes 6148
  15.1 15.2 %copy-start = (bf16[512,1024]{1,0:T(8,128)(2,1)S(1)}, bf16[512,1024]{1,0:T(8,128)(2,1)}, u32[]{:S(2)}) copy-start(bf16[512,1024]{1,0:T(8,128)(2,1)} %refs_15_.1) | copy-start | bytes 3145732
  18.4 11.9 %copy-start.1 = (bf16[640,640]{1,0:T(8,128)(2,1)S(1)}, bf16[640,640]{1,0:T(8,128)(2,1)}, u32[]{:S(2)}) copy-start(bf16[640,640]{1,0:T(8,128)(2,1)} %refs_14_.1) | copy-start | bytes 2457604
  18.4 7.5 %collective-permute-start.12 = (bf16[48,16,128]{2,1,0:T(8,128)(2,1)S(1)}, bf16[48,16,128]{2,1,0:T(8,128)(2,1)S(1)}, u32[]{:S(2)}, u32[]{:S(2)}) collective-permute-start(bf16[48,16,128]{2,1,0:T(8,128)(2,1)S(1)} %constant_dynamic-update-slice_fusion.refs_1_.refs_7_), channel_id=1, source_target_pairs={{0,2},{1,3},{2,0},{3,1},{4,6},{5,7},{6,4},{7,5},{8,10},{9,11},{10,... | collective-permute-start | bytes 589832 | tf_op jit(solution)/shard_map/ppermute | solution.py:402
  19.7 5.0 %collective-permute-start.4 = (bf16[27,16,128]{2,1,0:T(8,128)(2,1)S(1)}, bf16[27,16,128]{2,1,0:T(8,128)(2,1)S(1)}, u32[]{:S(2)}, u32[]{:S(2)}) collective-permute-start(bf16[27,16,128]{2,1,0:T(8,128)(2,1)S(1)} %pad_maximum_fusion.refs_0_), channel_id=1, source_target_pairs={{0,1},{1,0},{2,3},{3,2},{4,5},{5,4},{6,7},{7,6},{8,9},{9,8},{10,11... | collective-permute-start | bytes 331784 | tf_op jit(solution)/shard_map/ppermute | solution.py:402
  20.6 1.5 %collective-permute-start.11 = (bf16[16,16,128]{2,1,0:T(8,128)(2,1)S(1)}, bf16[16,16,128]{2,1,0:T(8,128)(2,1)S(1)}, u32[]{:S(2)}, u32[]{:S(2)}) collective-permute-start(bf16[16,16,128]{2,1,0:T(8,128)(2,1)S(1)} %pad_maximum_fusion.1.refs_0_.refs_6_), channel_id=1, source_target_pairs={{0,2},{1,3},{2,0},{3,1},{4,6},{5,7},{6,4},{7,5},{8,10},{9,11},{10,... | collective-permute-start | bytes 196616 | tf_op jit(solution)/shard_map/ppermute | solution.py:402
  20.6 8.9 %collective-permute-start.2 = (bf16[27,16,128]{2,1,0:T(8,128)(2,1)S(1)}, bf16[27,16,128]{2,1,0:T(8,128)(2,1)S(1)}, u32[]{:S(2)}, u32[]{:S(2)}) collective-permute-start(bf16[27,16,128]{2,1,0:T(8,128)(2,1)S(1)} %pad_maximum_fusion.refs_0_), channel_id=1, source_target_pairs={{0,2},{1,3},{2,0},{3,1},{4,6},{5,7},{6,4},{7,5},{8,10},{9,11},{10,... | collective-permute-start | bytes 331784 | tf_op jit(solution)/shard_map/ppermute | solution.py:402
  21.1 8.3 %collective-permute-start.3 = (bf16[27,16,128]{2,1,0:T(8,128)(2,1)S(1)}, bf16[27,16,128]{2,1,0:T(8,128)(2,1)S(1)}, u32[]{:S(2)}, u32[]{:S(2)}) collective-permute-start(bf16[27,16,128]{2,1,0:T(8,128)(2,1)S(1)} %pad_maximum_fusion.refs_0_), channel_id=1, source_target_pairs={{0,6},{1,7},{2,4},{3,5},{4,2},{5,3},{6,0},{7,1},{8,14},{9,15},{10,... | collective-permute-start | bytes 331784 | tf_op jit(solution)/shard_map/ppermute | solution.py:402
  22.1 7.4 %collective-permute-start.6 = (bf16[27,16,128]{2,1,0:T(8,128)(2,1)S(1)}, bf16[27,16,128]{2,1,0:T(8,128)(2,1)S(1)}, u32[]{:S(2)}, u32[]{:S(2)}) collective-permute-start(bf16[27,16,128]{2,1,0:T(8,128)(2,1)S(1)} %pad_maximum_fusion.refs_0_), channel_id=1, source_target_pairs={{0,7},{1,6},{2,5},{3,4},{4,3},{5,2},{6,1},{7,0},{8,15},{9,14},{10,... | collective-permute-start | bytes 331784 | tf_op jit(solution)/shard_map/ppermute | solution.py:402
  24.7 4.7 %collective-permute-start.5 = (bf16[27,16,128]{2,1,0:T(8,128)(2,1)S(1)}, bf16[27,16,128]{2,1,0:T(8,128)(2,1)S(1)}, u32[]{:S(2)}, u32[]{:S(2)}) collective-permute-start(bf16[27,16,128]{2,1,0:T(8,128)(2,1)S(1)} %collective-permute-done.4.refs_3_), channel_id=1, source_target_pairs={{0,2},{1,3},{2,0},{3,1},{4,6},{5,7},{6,4},{7,5},{8,10},{9,11},{10,... | collective-permute-start | bytes 331784 | tf_op jit(solution)/shard_map/ppermute | solution.py:402
  28.9 1.4 %collective-permute-start.13 = (f32[3,16,128]{2,1,0:T(8,128)S(1)}, f32[3,16,128]{2,1,0:T(8,128)S(1)}, u32[]{:S(2)}, u32[]{:S(2)}) collective-permute-start(f32[3,16,128]{2,1,0:T(8,128)S(1)} %get-tuple-element.16), channel_id=1, source_target_pairs={{0,2},{1,3},{2,0},{3,1},{4,6},{5,7},{6,4},{7,5},{8,10},{9,11},{10,... | collective-permute-start | bytes 73736 | tf_op jit(solution)/shard_map/ppermute | solution.py:402
